TPU v7x, 256 devices: a whole 4x4x8 slice. The times are simulated.
256 devices in a mesh: segment: 4 (over z_hi, core), dp: 16 (over z_lo, y), mp: 4 (over x).
Axes of the slice: x: 4, y: 4, z: 8 (z_hi: 2, z_lo: 4; z = z_hi * 4 + z_lo), core: 2. Of those that a mesh axis runs over, the one named last changes fastest.
Arguments:
- hidden: bfloat16 [384, 64, 4096], P(('segment', 'dp'))
- final_gain: bfloat16 [4096], replicated, may hold values from 0.099609375 to 1.8984375
- key_weight: bfloat16 [4096, 2048], P('dp', 'mp'), may hold values from -0.09375 to 0.09375
- value_weight: bfloat16 [4096, 2048], P('dp', 'mp'), may hold values from -0.09375 to 0.09375
- queries: bfloat16 [32, 128, 2048], P('dp', None, 'mp'), may hold values from -6 to 6
- context_grad: bfloat16 [32, 128, 2048], P('dp', None, 'mp'), may hold values from -384 to 384
- passage_count: int32 [32], replicated, may hold values from 4 to 16, as said below
- passage_slot: int32 [32, 16], replicated, may hold values from -1 to 287, as said below
- slot_question: int32 [32], replicated, may hold values from 0 to 31, as said below
Outputs:
- grad_hidden: bfloat16 [384, 64, 4096], P(('segment', 'dp'), 'mp')
Inputs may be any that keep to these rules, and one draw needn't show every extreme that they name: `passage_count`: the counts add up to 288, and some question has 16 passages. `passage_slot`: entry [q, j] is the slot holding passage j of question q for j below passage_count[q], and -1 beyond. Slots are numbered device by device in the order of the segment and dp indices, 6 to a device; only devices of the first three segment indices hold passages, each of their slots exactly one, and no slot is named twice. One device holds at most 1 passages of the questions served by the decoder rows of one dp index (rows 2 * c to 2 * c + 1 on dp index c), and one segment index at most 6 passages of one question; both bounds are reached. `slot_question`: A permutation.
All inputs are finite; a program needn't handle non-finite values.
Results may differ from a plain program's by a relative error of at most 0.015.
Values may be sent and summed in bfloat16 or wider, within the bound.
A program may use at most 128 MiB of HBM per device.

v0:
```python
import math
import jax
import jax.numpy as jnp
from jax import lax
from jax.sharding import PartitionSpec as P

HEAD_DIM = 64
EPSILON = 1e-06


def on_device(
    hidden,
    final_gain,
    key_weight,
    value_weight,
    queries,
    context_grad,
    passage_count,
    passage_slot,
    slot_question,
):
    segments = lax.axis_size("segment")
    columns = lax.axis_size("dp")
    tensor_ways = lax.axis_size("mp")
    segment_at = lax.axis_index("segment")
    column_at = lax.axis_index("dp")
    tensor_at = lax.axis_index("mp")
    slots_here = hidden.shape[0]
    seq_len = hidden.shape[1]
    model_width = hidden.shape[2]
    questions = passage_count.shape[0]
    most_passages = passage_slot.shape[1]
    q_here = queries.shape[0]
    target_len = queries.shape[1]
    encoders = (segments - 1) * columns
    per_device = (q_here * most_passages + encoders - 1) // encoders
    per_segment = (most_passages + segments - 2) // (segments - 1)
    inner_here = key_weight.shape[1]
    heads_here = inner_here // HEAD_DIM
    row_count = slots_here * seq_len
    scaling = 1.0 / math.sqrt(HEAD_DIM)
    key_full, value_full = (
        lax.all_gather(key_weight, "dp", axis=0, tiled=True),
        lax.all_gather(value_weight, "dp", axis=0, tiled=True),
    )

    def project(normed_rows, weight_full):
        return jnp.dot(normed_rows, weight_full, preferred_element_type=jnp.float32)

    def project_back(grad_rows, weight_full):
        return lax.dot_general(
            grad_rows, weight_full, (((1,), (1,)), ((), ())), preferred_element_type=jnp.float32
        )

    hidden_rows = hidden.reshape(row_count, model_width)
    gain_vec = final_gain.astype(jnp.float32)
    inv_rms = lax.rsqrt(
        jnp.mean(jnp.square(hidden_rows.astype(jnp.float32)), axis=-1, keepdims=True) + EPSILON
    )
    normed = (hidden_rows.astype(jnp.float32) * inv_rms * gain_vec).astype(jnp.bfloat16)
    key_rows = project(normed, key_full).astype(jnp.bfloat16)
    value_rows = project(normed, value_full).astype(jnp.bfloat16)
    packed = jnp.concatenate([key_rows, value_rows], axis=-1).reshape(
        slots_here, seq_len, 2 * inner_here
    )
    question_ids = jnp.arange(questions, dtype=jnp.int32)
    passage_ids = jnp.arange(most_passages, dtype=jnp.int32)
    home_row = jnp.sum(
        jnp.where(slot_question[None, :] == question_ids[:, None], question_ids[None, :], 0), axis=1
    )
    present = (passage_slot >= 0) & (passage_ids[None, :] < passage_count[:, None])
    local_ids = jnp.arange(slots_here, dtype=jnp.int32)
    my_slots = (segment_at * columns + column_at) * slots_here + local_ids
    matched = (passage_slot[None, :, :] == my_slots[:, None, None]) & present[None, :, :]
    holding = jnp.any(matched, axis=(1, 2))
    owner_question = jnp.sum(jnp.where(matched, question_ids[None, :, None], 0), axis=(1, 2))
    owner_row = jnp.sum(
        jnp.where(owner_question[:, None] == question_ids[None, :], home_row[None, :], 0), axis=1
    )
    target_column = owner_row // q_here
    earlier = (
        holding[None, :]
        & (target_column[None, :] == target_column[:, None])
        & (local_ids[None, :] < local_ids[:, None])
    )
    send_rank = jnp.sum(earlier.astype(jnp.int32), axis=1)
    send_pick = (
        holding[None, None, :]
        & (target_column[None, None, :] == jnp.arange(columns, dtype=jnp.int32)[:, None, None])
        & (send_rank[None, None, :] == jnp.arange(per_device, dtype=jnp.int32)[None, :, None])
    ).astype(jnp.bfloat16)
    outgoing = jnp.einsum(
        "gcl,lsx->gcsx", send_pick, packed, preferred_element_type=jnp.float32
    ).astype(jnp.bfloat16)
    incoming = lax.all_to_all(outgoing, "dp", split_axis=0, concat_axis=0, tiled=True)
    row_ids = column_at * q_here + jnp.arange(q_here, dtype=jnp.int32)
    my_questions = jnp.sum(
        jnp.where(row_ids[:, None] == question_ids[None, :], slot_question[None, :], 0), axis=1
    )
    is_mine = my_questions[:, None] == question_ids[None, :]
    row_slots = jnp.sum(
        jnp.where(is_mine[:, :, None], passage_slot[None, :, :], 0), axis=1
    ).reshape(-1)
    row_live = jnp.any(is_mine[:, :, None] & present[None, :, :], axis=1).reshape(-1)
    question_of = jnp.repeat(jnp.arange(q_here, dtype=jnp.int32), most_passages)
    segment_slots = columns * slots_here
    segment_of = row_slots // segment_slots
    column_key = row_slots % segment_slots
    source_of = column_key // slots_here
    on_segment = row_live & (segment_of == segment_at)
    ahead = on_segment[None, :] & (column_key[None, :] < column_key[:, None])
    segment_rank = jnp.sum(
        (ahead & (question_of[None, :] == question_of[:, None])).astype(jnp.int32), axis=1
    )
    device_rank = jnp.sum(
        (ahead & (source_of[None, :] == source_of[:, None])).astype(jnp.int32), axis=1
    )
    gather_pick = jnp.sum(
        (
            on_segment[:, None, None, None, None]
            & (
                question_of[:, None, None, None, None]
                == jnp.arange(q_here, dtype=jnp.int32)[None, :, None, None, None]
            )
            & (
                segment_rank[:, None, None, None, None]
                == jnp.arange(per_segment, dtype=jnp.int32)[None, None, :, None, None]
            )
            & (
                source_of[:, None, None, None, None]
                == jnp.arange(columns, dtype=jnp.int32)[None, None, None, :, None]
            )
            & (
                device_rank[:, None, None, None, None]
                == jnp.arange(per_device, dtype=jnp.int32)[None, None, None, None, :]
            )
        ).astype(jnp.int32),
        axis=0,
    ).astype(jnp.bfloat16)
    compact = jnp.einsum(
        "krgc,gcsx->krsx", gather_pick, incoming, preferred_element_type=jnp.float32
    ).astype(jnp.bfloat16)
    pooled = lax.all_gather(compact[None], "segment", axis=0, tiled=True)
    segment_counts = jnp.sum(
        (
            row_live[None, None, :]
            & (question_of[None, None, :] == jnp.arange(q_here, dtype=jnp.int32)[:, None, None])
            & (segment_of[None, None, :] == jnp.arange(segments, dtype=jnp.int32)[None, :, None])
        ).astype(jnp.int32),
        axis=2,
    )
    live_slots = (
        jnp.arange(per_segment, dtype=jnp.int32)[None, None, :] < segment_counts[:, :, None]
    )
    key_total = segments * per_segment * seq_len
    key_live = (
        jnp.broadcast_to(live_slots[:, :, :, None], (q_here, segments, per_segment, seq_len))
        .reshape(q_here, key_total)
        .astype(jnp.float32)
    )

    def head_pass(head_no):
        first_col = head_no * HEAD_DIM
        key_head = lax.dynamic_slice_in_dim(pooled, first_col, HEAD_DIM, 4)
        value_head = lax.dynamic_slice_in_dim(pooled, inner_here + first_col, HEAD_DIM, 4)
        query_head = lax.dynamic_slice_in_dim(queries, first_col, HEAD_DIM, 2)
        grad_head = lax.dynamic_slice_in_dim(context_grad, first_col, HEAD_DIM, 2)
        scores = jnp.einsum(
            "ktd,skrld->ktsrl", query_head, key_head, preferred_element_type=jnp.float32
        )
        scores = scores.reshape(q_here, target_len, key_total) * scaling
        weights = jnp.exp(scores) * key_live[:, None, :]
        attn_probs = weights / jnp.sum(weights, axis=-1, keepdims=True)
        probs_half = attn_probs.astype(jnp.bfloat16).reshape(
            q_here, target_len, segments, per_segment, seq_len
        )
        context = jnp.einsum(
            "ktsrl,skrld->ktd", probs_half, value_head, preferred_element_type=jnp.float32
        ).astype(jnp.bfloat16)
        row_delta = jnp.sum(
            grad_head.astype(jnp.float32) * context.astype(jnp.float32), axis=-1, keepdims=True
        )
        prob_grads = jnp.einsum(
            "ktd,skrld->ktsrl", grad_head, value_head, preferred_element_type=jnp.float32
        )
        prob_grads = prob_grads.reshape(q_here, target_len, key_total)
        score_grads = (attn_probs * (prob_grads - row_delta)).astype(jnp.bfloat16)
        score_grads = score_grads.reshape(q_here, target_len, segments, per_segment, seq_len)
        score_mine = lax.dynamic_index_in_dim(score_grads, segment_at, 2, keepdims=False)
        probs_mine = lax.dynamic_index_in_dim(probs_half, segment_at, 2, keepdims=False)
        key_grads = (
            jnp.einsum("ktrl,ktd->krld", score_mine, query_head, preferred_element_type=jnp.float32)
            * scaling
        ).astype(jnp.bfloat16)
        value_grads = jnp.einsum(
            "ktrl,ktd->krld", probs_mine, grad_head, preferred_element_type=jnp.float32
        ).astype(jnp.bfloat16)
        return (key_grads, value_grads)

    key_grads, value_grads = lax.map(head_pass, jnp.arange(heads_here, dtype=jnp.int32))
    grad_shape = (q_here, per_segment, seq_len, inner_here)
    key_grads = jnp.moveaxis(key_grads, 0, 3).reshape(grad_shape)
    value_grads = jnp.moveaxis(value_grads, 0, 3).reshape(grad_shape)
    my_share = jnp.concatenate([key_grads, value_grads], axis=-1)
    spread_back = jnp.einsum(
        "krgc,krsx->gcsx", gather_pick, my_share, preferred_element_type=jnp.float32
    ).astype(jnp.bfloat16)
    owner_back = lax.all_to_all(spread_back, "dp", split_axis=0, concat_axis=0, tiled=True)
    token_grads = jnp.einsum(
        "gcl,gcsx->slx", send_pick, owner_back, preferred_element_type=jnp.float32
    ).astype(jnp.bfloat16)
    grad_flat = token_grads.reshape(row_count, 2 * inner_here)
    my_rows = row_count // tensor_ways
    token_share = seq_len // tensor_ways
    normed_grad = lax.psum_scatter(
        (
            project_back(grad_flat[:, :inner_here], key_full)
            + project_back(grad_flat[:, inner_here:], value_full)
        ).astype(jnp.bfloat16),
        "mp",
        scatter_dimension=0,
        tiled=True,
    ).astype(jnp.float32)
    first_token = tensor_at * token_share
    states_mine = lax.dynamic_slice_in_dim(hidden, first_token, token_share, 1).astype(jnp.float32)
    states_mine = states_mine.transpose(1, 0, 2).reshape(my_rows, model_width)
    rms_mine = lax.dynamic_slice_in_dim(
        inv_rms.reshape(slots_here, seq_len, 1), first_token, token_share, 1
    )
    rms_mine = rms_mine.transpose(1, 0, 2).reshape(my_rows, 1)
    scaled = gain_vec * normed_grad
    hidden_grad = rms_mine * scaled - states_mine * rms_mine**3 * jnp.mean(
        states_mine * scaled, axis=-1, keepdims=True
    )
    hidden_grad = hidden_grad.reshape(token_share, slots_here, model_width).transpose(1, 0, 2)
    return hidden_grad.astype(jnp.bfloat16)


def solution(mesh):
    in_specs = (
        P(("segment", "dp"), None, None),
        P(),
        P("dp", "mp"),
        P("dp", "mp"),
        P("dp", None, "mp"),
        P("dp", None, "mp"),
        P(),
        P(),
        P(),
    )
    out_specs = P(("segment", "dp"), "mp", None)
    return jax.shard_map(
        on_device, mesh=mesh, in_specs=in_specs, out_specs=out_specs, check_vma=False
    )
```

profile of v0, /device:TPU:1, one launch (start us, length us, event | category | flops | bytes accessed | tf_op | source)
XLA Modules:
  0.0 518.2 jit_solution(18247863727032568012)
XLA Ops:
  8.0 0.7 convert_element_type.146
  8.7 2.6 multiply_reduce_fusion
  13.1 2.7 fusion.34
  15.8 75.3 %all-gather.7.cloned.1.call-done = bf16[4096,512]{1,0:T(8,128)(2,1)} async-done(((bf16[256,512]{1,0:T(8,128)(2,1)}), bf16[4096,512]{1,0:T(8,128)(2,1)}) %all-gather.7.cloned.1.call-update) | async-done | bytes 4194320 | tf_op jit(solution)/shard_map/all_gather | solution.py:44
  91.1 4.9 convolution_convert_fusion.1
  96.0 82.6 %all-gather.5.cloned.1.call-done = bf16[4096,512]{1,0:T(8,128)(2,1)} async-done(((bf16[256,512]{1,0:T(8,128)(2,1)}), bf16[4096,512]{1,0:T(8,128)(2,1)}) %all-gather.5.cloned.1.call-update) | async-done | bytes 4194320 | tf_op jit(solution)/shard_map/all_gather | solution.py:43
  178.6 4.0 convolution_convert_fusion.2
  182.7 0.9 convert_bitcast_fusion
  183.7 2.5 copy.68
  186.2 5.6 %all-to-all-start = ((bf16[16,1,64,1024]{3,2,1,0:T(8,128)(2,1)}), bf16[16,1,64,1024]{3,2,1,0:T(8,128)(2,1)S(1)}, u32[]{:S(2)}, u32[]{:S(2)}) async-start(bf16[16,1,64,1024]{3,2,1,0:T(8,128)(2,1)} %copy.68), calls=%async_computation | async-start | bytes 4194304 | tf_op jit(solution)/shard_map/all_to_all | solution.py:95
  193.4 35.5 %all-to-all-done = bf16[16,1,64,1024]{3,2,1,0:T(8,128)(2,1)S(1)} async-done(((bf16[16,1,64,1024]{3,2,1,0:T(8,128)(2,1)}), bf16[16,1,64,1024]{3,2,1,0:T(8,128)(2,1)S(1)}, u32[]{:S(2)}, u32[]{:S(2)}) %all-to-all-start) | async-done | bytes 2097184 | tf_op jit(solution)/shard_map/all_to_all | solution.py:95
  228.9 1.5 fusion.44
  230.5 2.0 copy.70
  233.4 99.8 %all-gather.9.cloned.1.call-done = bf16[8,6,64,1024]{3,2,1,0:T(8,128)(2,1)} async-done(((bf16[2,6,64,1024]{3,2,1,0:T(8,128)(2,1)}), bf16[8,6,64,1024]{3,2,1,0:T(8,128)(2,1)}) %all-gather.9.cloned.1.call-update) | async-done | bytes 6291472 | tf_op jit(solution)/shard_map/all_gather | solution.py:143
  333.2 6.7 %copy.72 = bf16[4,2,6,64,1024]{4,3,2,0,1:T(8,128)(2,1)} copy(bf16[4,2,6,64,1024]{4,3,2,1,0:T(8,128)(2,1)} %bitcast.142) | data formatting | bytes 12582912
  339.9 57.2 %while.15 = (s32[]{:T(128)}, bf16[8,2,6,64,64]{4,3,2,1,0:T(8,128)(2,1)}, bf16[8,2,6,64,64]{4,3,2,1,0:T(8,128)(2,1)}, s32[8]{0:T(128)S(1)}, bf16[2,128,512]{1,2,0...) while((s32[]{:T(128)}, ...), condition=%wide.region_16.17_spmd.clone, body=%wide.region_13.16_spmd.clone.sunk | while | flops 178650624 | bytes 12167454 | solution.py:200
  341.1 1.6 fusion.113
  343.1 1.4 constant_dynamic-slice_fusion.2
  345.3 0.9 fusion.116
  346.2 0.9 fusion.117
  348.2 1.6 fusion.113
  350.2 1.4 constant_dynamic-slice_fusion.2
  352.5 0.9 fusion.116
  353.3 0.9 fusion.117
  355.4 1.6 fusion.113
  357.4 1.4 constant_dynamic-slice_fusion.2
  359.6 0.9 fusion.116
  360.5 0.9 fusion.117
  362.5 1.6 fusion.113
  364.5 1.4 constant_dynamic-slice_fusion.2
  366.8 0.9 fusion.116
  367.6 0.9 fusion.117
  369.7 1.6 fusion.113
  371.7 1.4 constant_dynamic-slice_fusion.2
  373.9 0.9 fusion.116
  374.8 0.9 fusion.117
  376.9 1.6 fusion.113
  378.8 1.4 constant_dynamic-slice_fusion.2
  381.1 0.9 fusion.116
  382.0 0.9 fusion.117
  384.0 1.6 fusion.113
  386.0 1.4 constant_dynamic-slice_fusion.2
  388.2 0.9 fusion.116
  389.1 0.9 fusion.117
  391.1 1.6 fusion.113
  393.1 1.4 constant_dynamic-slice_fusion.2
  395.4 0.9 fusion.116
  396.3 0.9 fusion.117
  397.1 2.4 copy.90
  399.6 1.0 reshape.670
  400.6 2.4 copy.91
  403.0 1.8 reshape.671
  404.8 2.4 fusion.47
  407.2 1.2 copy.78
  408.4 51.3 %all_to_all.10 = bf16[16,1,64,1024]{3,2,1,0:T(8,128)(2,1)S(1)} all-to-all(bf16[16,1,64,1024]{3,2,1,0:T(8,128)(2,1)S(1)} %copy.78), channel_id=1, replica_groups=mesh['segment'=4,'dp'=16,'mp'=4] {'dp'}, dimensions={0} | all-to-all | bytes 4194304 | tf_op jit(solution)/shard_map/all_to_all | solution.py:208
  459.7 1.3 fusion.53
  461.3 4.2 fusion.58
  465.5 3.5 add_convert_fusion
  469.0 1.3 convert_bitcast_fusion.1
  470.3 2.3 copy.80
  472.6 1.7 reshape.658
  474.6 33.6 %reduce-scatter.2.cloned.1.call-done = bf16[96,4096]{1,0:T(8,128)(2,1)} async-done(((bf16[384,4096]{1,0:T(8,128)(2,1)}), bf16[96,4096]{1,0:T(8,128)(2,1)}) %reduce-scatter.2.cloned.1.call-update) | async-done | bytes 786448 | tf_op jit(solution)/shard_map/reduce_scatter | solution.py:215
  508.1 1.5 multiply_reduce_fusion.1
  510.4 1.3 copy.81
  (137 shorter events, 20.5 us)
Async XLA Ops:
  6.5 6.6 %copy-start = (bf16[6,64,4096]{2,1,0:T(8,128)(2,1)S(1)}, bf16[6,64,4096]{2,1,0:T(8,128)(2,1)}, u32[]{:S(2)}) copy-start(bf16[6,64,4096]{2,1,0:T(8,128)(2,1)} %param.11) | copy-start | bytes 9437188
  6.5 4.9 copy-start.21
  6.5 5.0 copy-start.6
  6.5 5.0 copy-start.20
  6.5 84.5 %all-gather.7.cloned.1.call-start = ((), (), s32[]{:S(2)}) async-start(), calls=%async_computation.4 | async-start | bytes 4456448 | tf_op jit(solution)/shard_map/all_gather | solution.py:44
  7.3 171.3 %all-gather.5.cloned.1.call-start = ((), (), s32[]{:S(2)}) async-start(), calls=%async_computation.3 | async-start | bytes 4456448 | tf_op jit(solution)/shard_map/all_gather | solution.py:43
  11.3 4.5 copy-start.8
  11.6 4.2 copy-start.10
  11.8 4.0 copy-start.12
  12.3 3.5 copy-start.15
  15.8 162.8 %copy-start.2 = (bf16[384,4096]{1,0:T(8,128)(2,1)S(1)}, bf16[384,4096]{1,0:T(8,128)(2,1)}, u32[]{:S(2)}) copy-start(bf16[384,4096]{1,0:T(8,128)(2,1)} %fusion.34) | copy-start | bytes 9437188
  178.6 4.1 copy-start.13
  178.6 4.1 copy-start.16
  178.6 4.1 copy-start.18
  186.2 5.7 %copy-start.22 = (s32[32]{0:T(128)S(1)}, s32[32]{0:T(128)}, u32[]{:S(2)}) copy-start(s32[32]{0:T(128)} %param.19) | copy-start | bytes 388
  186.2 6.0 %copy-start.7 = (s32[32,16]{0,1:T(8,128)S(1)}, s32[32,16]{0,1:T(8,128)}, u32[]{:S(2)}) copy-start(s32[32,16]{0,1:T(8,128)} %param.18) | copy-start | bytes 6148
  186.2 6.2 %copy-start.11 = (pred[32,16]{0,1:T(8,128)(4,1)S(1)}, pred[32,16]{0,1:T(8,128)(4,1)}, u32[]{:S(2)}) copy-start(pred[32,16]{0,1:T(8,128)(4,1)} %copy-done.10) | copy-start | bytes 1540
  186.2 42.8 %all-to-all-start = ((bf16[16,1,64,1024]{3,2,1,0:T(8,128)(2,1)}), bf16[16,1,64,1024]{3,2,1,0:T(8,128)(2,1)S(1)}, u32[]{:S(2)}, u32[]{:S(2)}) async-start(bf16[16,1,64,1024]{3,2,1,0:T(8,128)(2,1)} %copy.68), calls=%async_computation | async-start | bytes 4194304 | tf_op jit(solution)/shard_map/all_to_all | solution.py:95
  191.8 141.4 %all-gather.9.cloned.1.call-start = ((), (), s32[]{:S(2)}) async-start(), calls=%async_computation.6 | async-start | bytes 7864320 | tf_op jit(solution)/shard_map/all_gather | solution.py:143
  230.5 2.3 copy-start.4
  230.5 2.5 copy-start.5
  232.5 275.6 %reduce-scatter.2.cloned.1.call-start = ((), (), s32[]{:S(2)}) async-start(), calls=%async_computation.5 | async-start | bytes 3932160 | tf_op jit(solution)/shard_map/reduce_scatter | solution.py:215
  408.4 51.3 %copy-start.14 = (pred[6]{0:T(512)(128)(4,1)S(1)}, pred[6]{0:T(512)(128)(4,1)}, u32[]{:S(2)}) copy-start(pred[6]{0:T(512)(128)(4,1)} %copy-done.12) | copy-start | bytes 22
  408.4 51.3 %copy-start.17 = (s32[6]{0:T(128)S(1)}, s32[6]{0:T(128)}, u32[]{:S(2)}) copy-start(s32[6]{0:T(128)} %copy-done.15) | copy-start | bytes 76
  408.4 51.3 %copy-start.19 = (pred[6]{0:T(512)(128)(4,1)S(1)}, pred[6]{0:T(512)(128)(4,1)}, u32[]{:S(2)}) copy-start(pred[6]{0:T(512)(128)(4,1)} %broadcast_compare_fusion) | copy-start | bytes 22
  461.3 4.2 copy-start.1
  472.6 1.7 copy-start.9
  508.1 1.5 copy-start.3
Sparse Core Ops, SparseCore 0:
  9.1 81.8 all-gather.6
  92.9 85.7 all-gather.4
  232.7 100.5 all-gather.8
  469.1 38.9 reduce-scatter.1
where the time goes:
time: 519 us; the launch traced here: 518 us
  waiting for transfers between devices  328 us (63%)
  matrix products  56.4 us (11%)
  blocking collectives  51.3 us (10%)
  local copies, waits for them, and re-layouts  43.2 us (8%)
  other arithmetic  14.6 us (3%)
  between operations  13.6 us (3%)
  starting transfers between devices  5.98 us (1%)
    all_gather x1, waiting for transfers between devices, on_device(): pooled = lax.all_gather(compact[None], 'segment', axis=0, tiled=True)  99.8 us
    all_gather x1, waiting for transfers between devices, on_device(): lax.all_gather(key_weight, 'dp', axis=0, tiled=True)  82.6 us
    all_gather x1, waiting for transfers between devices, on_device(): lax.all_gather(value_weight, 'dp', axis=0, tiled=True)  75.3 us
    all_to_all x1, blocking collectives, on_device(): lax.all_to_all(spread_back, 'dp', split_axis=0, concat_axis=0, tiled=True)  51.3 us
    all_to_all x1, waiting for transfers between devices, on_device(): lax.all_to_all(outgoing, 'dp', split_axis=0, concat_axis=0, tiled=True)  35.5 us
    reduce_scatter x1, waiting for transfers between devices, on_device(): lax.psum_scatter((project_back(grad_flat[:, :inner_here], key_full) + pro...  33.6 us
    dot_general x8, matrix products, head_pass(): jnp.einsum('ktd,skrld->ktsrl', query_head, key_head, preferred_element_ty...  13.2 us
    dynamic_slice x8, local copies, waits for them, and re-layouts, head_pass(): lax.dynamic_slice_in_dim(pooled, inner_here + first_col, HEAD_DIM, 4)  11.4 us
  transfers between devices with their start and end apart: 5, of which 5 were waited for; matrix products, arithmetic and copies ran while one was open for 4% of the time, Pallas kernels for 0%

commit v1 on v0

--- a/solution.py
+++ b/solution.py
@@ -41,7 +41,9 @@
     scaling = 1.0 / math.sqrt(HEAD_DIM)
     key_full, value_full = (
         lax.all_gather(key_weight, "dp", axis=0, tiled=True),
-        lax.all_gather(value_weight, "dp", axis=0, tiled=True),
+        jnp.concatenate(
+            lax.all_to_all(jnp.stack([value_weight] * lax.axis_size("dp")), "dp", 0, 0), axis=0
+        ),
     )
 
     def project(normed_rows, weight_full):

time: 519 us -> 504 us (0.971)
  waiting for transfers between devices: 328 us -> 281 us
  starting transfers between devices: 5.98 us -> 31.4 us
    all_to_all x0 -> x1, waiting for transfers between devices: none -> 108 us  [on_device(): lax.all_to_all(jnp.stack([value_weight] * lax.axis_size('dp')), 'dp', 0, 0)]
    all_gather x1, waiting for transfers between devices: 82.6 us -> 2.12 us  [on_device(): lax.all_gather(key_weight, 'dp', axis=0, tiled=True)]
    all_gather x1 -> x0, waiting for transfers between devices: 75.3 us -> none  [on_device(): lax.all_gather(value_weight, 'dp', axis=0, tiled=True)]
    all_to_all x1, starting transfers between devices: 5.65 us -> 21.6 us  [on_device(): lax.all_to_all(outgoing, 'dp', split_axis=0, concat_axis=0, tiled=True)]
    all_to_all x0 -> x1, starting transfers between devices: none -> 9.49 us  [on_device(): lax.all_to_all(jnp.stack([value_weight] * lax.axis_size('dp')), 'dp', 0, 0)]
where the time goes in v1:
time: 504 us; the launch traced here: 502 us
  waiting for transfers between devices  281 us (56%)
  matrix products  58.6 us (12%)
  blocking collectives  51.3 us (10%)
  local copies, waits for them, and re-layouts  46.9 us (9%)
  starting transfers between devices  31.4 us (6%)
  other arithmetic  14.8 us (3%)
  between operations  13.6 us (3%)
    all_to_all x1, waiting for transfers between devices, on_device(): lax.all_to_all(jnp.stack([value_weight] * lax.axis_size('dp')), 'dp', 0, 0)  108 us
    all_gather x1, waiting for transfers between devices, on_device(): pooled = lax.all_gather(compact[None], 'segment', axis=0, tiled=True)  96.5 us
    all_to_all x1, blocking collectives, on_device(): lax.all_to_all(spread_back, 'dp', split_axis=0, concat_axis=0, tiled=True)  51.3 us
    all_to_all x1, waiting for transfers between devices, on_device(): lax.all_to_all(outgoing, 'dp', split_axis=0, concat_axis=0, tiled=True)  39.9 us
    reduce_scatter x1, waiting for transfers between devices, on_device(): lax.psum_scatter((project_back(grad_flat[:, :inner_here], key_full) + pro...  33.6 us
    all_to_all x1, starting transfers between devices, on_device(): lax.all_to_all(outgoing, 'dp', split_axis=0, concat_axis=0, tiled=True)  21.6 us
    dot_general x8, matrix products, head_pass(): jnp.einsum('ktd,skrld->ktsrl', query_head, key_head, preferred_element_ty...  13.2 us
    dynamic_slice x8, local copies, waits for them, and re-layouts, head_pass(): lax.dynamic_slice_in_dim(pooled, inner_here + first_col, HEAD_DIM, 4)  11.4 us
  transfers between devices with their start and end apart: 5, of which 5 were waited for; matrix products, arithmetic and copies ran while one was open for 4% of the time, Pallas kernels for 0%

profile of v1, /device:TPU:1, one launch (start us, length us, event | category | flops | bytes accessed | tf_op | source)
XLA Modules:
  0.0 502.3 jit_solution(12956226049567279889)
XLA Ops:
  6.5 3.3 stack.2
  9.8 9.5 %all-to-all-start = ((bf16[16,256,512]{2,1,0:T(8,128)(2,1)}), bf16[16,256,512]{2,1,0:T(8,128)(2,1)}, u32[]{:S(2)}, u32[]{:S(2)}) async-start(bf16[16,256,512]{2,1,0:T(8,128)(2,1)} %stack.2), calls=%async_computation | async-start | bytes 8388608 | tf_op jit(solution)/shard_map/all_to_all | solution.py:45
  23.0 2.7 fusion.34
  25.7 2.7 multiply_convert_fusion
  28.5 107.9 %all-to-all-done = bf16[16,256,512]{2,1,0:T(8,128)(2,1)} async-done(((bf16[16,256,512]{2,1,0:T(8,128)(2,1)}), bf16[16,256,512]{2,1,0:T(8,128)(2,1)}, u32[]{:S(2)}, u32[]{:S(2)}) %all-to-all-start) | async-done | bytes 4194336 | tf_op jit(solution)/shard_map/all_to_all | solution.py:45
  136.3 5.1 %convolution_convert_fusion.1 = bf16[384,512]{1,0:T(8,128)(2,1)S(1)} fusion(bf16[384,4096]{1,0:T(8,128)(2,1)} %bitcast.147, bf16[4096,512]{1,0:T(8,128)(2,1)} %bitcast.8), kind=kOutput, calls=%fused_computation.64 | convolution fusion | flops 1610809344 | bytes 7733248 | tf_op jit(solution)/shard_map/dot_general | solution.py:50
  141.5 2.1 all-gather.4.cloned.1.call-done
  143.6 4.0 convolution_convert_fusion.2
  147.7 0.9 convert_bitcast_fusion
  148.6 2.5 copy.68
  151.1 21.6 %all-to-all-start.1 = ((bf16[16,1,64,1024]{3,2,1,0:T(8,128)(2,1)}), bf16[16,1,64,1024]{3,2,1,0:T(8,128)(2,1)S(1)}, u32[]{:S(2)}, u32[]{:S(2)}) async-start(bf16[16,1,64,1024]{3,2,1,0:T(8,128)(2,1)} %copy.68), calls=%async_computation.1 | async-start | bytes 4194304 | tf_op jit(solution)/shard_map/all_to_all | solution.py:97
  174.4 39.9 %all-to-all-done.1 = bf16[16,1,64,1024]{3,2,1,0:T(8,128)(2,1)S(1)} async-done(((bf16[16,1,64,1024]{3,2,1,0:T(8,128)(2,1)}), bf16[16,1,64,1024]{3,2,1,0:T(8,128)(2,1)S(1)}, u32[]{:S(2)}, u32[]{:S(2)}) %all-to-all-start.1) | async-done | bytes 2097184 | tf_op jit(solution)/shard_map/all_to_all | solution.py:97
  214.3 1.5 fusion.44
  215.9 2.0 copy.70
  218.8 96.5 %all-gather.6.cloned.1.call-done = bf16[8,6,64,1024]{3,2,1,0:T(8,128)(2,1)} async-done(((bf16[2,6,64,1024]{3,2,1,0:T(8,128)(2,1)}), bf16[8,6,64,1024]{3,2,1,0:T(8,128)(2,1)}) %all-gather.6.cloned.1.call-update) | async-done | bytes 6291472 | tf_op jit(solution)/shard_map/all_gather | solution.py:145
  315.2 6.7 %copy.72 = bf16[4,2,6,64,1024]{4,3,2,0,1:T(8,128)(2,1)} copy(bf16[4,2,6,64,1024]{4,3,2,1,0:T(8,128)(2,1)} %bitcast.144) | data formatting | bytes 12582912
  321.9 57.2 %while.15 = (s32[]{:T(128)}, bf16[8,2,6,64,64]{4,3,2,1,0:T(8,128)(2,1)}, bf16[8,2,6,64,64]{4,3,2,1,0:T(8,128)(2,1)}, s32[8]{0:T(128)S(1)}, bf16[2,128,512]{1,2,0...) while((s32[]{:T(128)}, ...), condition=%wide.region_16.17_spmd.clone, body=%wide.region_13.16_spmd.clone.sunk | while | flops 178650624 | bytes 12167454 | solution.py:202
  323.1 1.6 fusion.113
  325.1 1.4 constant_dynamic-slice_fusion.2
  327.3 0.9 fusion.116
  328.2 0.9 fusion.117
  330.3 1.6 fusion.113
  332.3 1.4 constant_dynamic-slice_fusion.2
  334.5 0.9 fusion.116
  337.4 1.6 fusion.113
  339.4 1.4 constant_dynamic-slice_fusion.2
  341.6 0.9 fusion.116
  342.5 0.9 fusion.117
  344.6 1.6 fusion.113
  346.5 1.4 constant_dynamic-slice_fusion.2
  348.8 0.9 fusion.116
  349.7 0.9 fusion.117
  351.7 1.6 fusion.113
  353.7 1.4 constant_dynamic-slice_fusion.2
  356.0 0.9 fusion.116
  356.9 0.9 fusion.117
  358.9 1.6 fusion.113
  360.9 1.4 constant_dynamic-slice_fusion.2
  363.1 0.9 fusion.116
  364.0 0.9 fusion.117
  366.0 1.6 fusion.113
  368.0 1.4 constant_dynamic-slice_fusion.2
  370.3 0.9 fusion.116
  371.1 0.9 fusion.117
  373.2 1.6 fusion.113
  375.2 1.4 constant_dynamic-slice_fusion.2
  377.4 0.9 fusion.116
  378.3 0.9 fusion.117
  379.2 2.4 copy.90
  381.6 1.0 reshape.686
  382.6 2.4 copy.91
  385.1 1.8 reshape.687
  386.9 2.4 fusion.47
  389.3 1.2 copy.78
  390.5 51.3 %all_to_all.15 = bf16[16,1,64,1024]{3,2,1,0:T(8,128)(2,1)S(1)} all-to-all(bf16[16,1,64,1024]{3,2,1,0:T(8,128)(2,1)S(1)} %copy.78), channel_id=1, replica_groups=mesh['segment'=4,'dp'=16,'mp'=4] {'dp'}, dimensions={0} | all-to-all | bytes 4194304 | tf_op jit(solution)/shard_map/all_to_all | solution.py:210
  441.8 1.3 fusion.53
  443.3 4.0 fusion.58
  447.4 5.7 %add_convert_fusion = bf16[384,4096]{1,0:T(8,128)(2,1)} fusion(f32[384,4096]{1,0:T(8,128)S(1)} %fusion.58, bf16[4096,512]{1,0:T(8,128)(2,1)} %bitcast.8, bf16[384,1024]{1,0:T(8,128)(2,1)S(1)} %reshape.669), kind=kOutput, calls=%fused_computation.42 | convolution fusion | flops 1613758464 | bytes 14024704 | tf_op jit(solution)/shard_map/dot_general | solution.py:53
  453.1 1.3 convert_bitcast_fusion.1
  454.4 2.3 copy.80
  456.7 1.7 reshape.674
  458.6 33.6 %reduce-scatter.2.cloned.1.call-done = bf16[96,4096]{1,0:T(8,128)(2,1)} async-done(((bf16[384,4096]{1,0:T(8,128)(2,1)}), bf16[96,4096]{1,0:T(8,128)(2,1)}) %reduce-scatter.2.cloned.1.call-update) | async-done | bytes 786448 | tf_op jit(solution)/shard_map/reduce_scatter | solution.py:217
  492.2 1.5 multiply_reduce_fusion.1
  494.4 1.3 copy.81
  (138 shorter events, 21.7 us)
Async XLA Ops:
  9.8 10.3 %copy-start.17 = (bf16[4096]{0:T(1024)(128)(2,1)S(1)}, bf16[4096]{0:T(1024)(128)(2,1)}, u32[]{:S(2)}) copy-start(bf16[4096]{0:T(1024)(128)(2,1)} %param.12) | copy-start | bytes 24580
  9.8 10.3 %copy-start = (bf16[6,64,4096]{2,1,0:T(8,128)(2,1)S(1)}, bf16[6,64,4096]{2,1,0:T(8,128)(2,1)}, u32[]{:S(2)}) copy-start(bf16[6,64,4096]{2,1,0:T(8,128)(2,1)} %param.11) | copy-start | bytes 9437188
  9.8 126.5 %all-to-all-start = ((bf16[16,256,512]{2,1,0:T(8,128)(2,1)}), bf16[16,256,512]{2,1,0:T(8,128)(2,1)}, u32[]{:S(2)}, u32[]{:S(2)}) async-start(bf16[16,256,512]{2,1,0:T(8,128)(2,1)} %stack.2), calls=%async_computation | async-start | bytes 8388608 | tf_op jit(solution)/shard_map/all_to_all | solution.py:45
  19.3 1.6 copy-start.21
  19.3 1.7 copy-start.5
  19.3 1.7 copy-start.20
  19.4 124.2 %all-gather.4.cloned.1.call-start = ((), (), s32[]{:S(2)}) async-start(), calls=%async_computation.4 | async-start | bytes 4456448 | tf_op jit(solution)/shard_map/all_gather | solution.py:43
  20.8 4.9 copy-start.7
  21.1 0.6 copy-start.9
  21.3 0.6 copy-start.11
  21.9 0.5 copy-start.14
  136.3 7.3 %copy-start.1 = (bf16[384,4096]{1,0:T(8,128)(2,1)S(1)}, bf16[384,4096]{1,0:T(8,128)(2,1)}, u32[]{:S(2)}) copy-start(bf16[384,4096]{1,0:T(8,128)(2,1)} %fusion.34) | copy-start | bytes 9437188
  143.6 4.1 copy-start.12
  143.6 4.1 copy-start.15
  143.6 4.1 copy-start.18
  151.1 21.7 %copy-start.22 = (s32[32]{0:T(128)S(1)}, s32[32]{0:T(128)}, u32[]{:S(2)}) copy-start(s32[32]{0:T(128)} %param.19) | copy-start | bytes 388
  151.1 22.0 %copy-start.6 = (s32[32,16]{0,1:T(8,128)S(1)}, s32[32,16]{0,1:T(8,128)}, u32[]{:S(2)}) copy-start(s32[32,16]{0,1:T(8,128)} %param.18) | copy-start | bytes 6148
  151.1 22.2 %copy-start.10 = (pred[32,16]{0,1:T(8,128)(4,1)S(1)}, pred[32,16]{0,1:T(8,128)(4,1)}, u32[]{:S(2)}) copy-start(pred[32,16]{0,1:T(8,128)(4,1)} %copy-done.9) | copy-start | bytes 1540
  151.1 63.2 %all-to-all-start.1 = ((bf16[16,1,64,1024]{3,2,1,0:T(8,128)(2,1)}), bf16[16,1,64,1024]{3,2,1,0:T(8,128)(2,1)S(1)}, u32[]{:S(2)}, u32[]{:S(2)}) async-start(bf16[16,1,64,1024]{3,2,1,0:T(8,128)(2,1)} %copy.68), calls=%async_computation.1 | async-start | bytes 4194304 | tf_op jit(solution)/shard_map/all_to_all | solution.py:97
  172.8 142.4 %all-gather.6.cloned.1.call-start = ((), (), s32[]{:S(2)}) async-start(), calls=%async_computation.6 | async-start | bytes 7864320 | tf_op jit(solution)/shard_map/all_gather | solution.py:145
  215.8 2.3 copy-start.3
  215.9 2.5 copy-start.4
  217.9 274.3 %reduce-scatter.2.cloned.1.call-start = ((), (), s32[]{:S(2)}) async-start(), calls=%async_computation.5 | async-start | bytes 3932160 | tf_op jit(solution)/shard_map/reduce_scatter | solution.py:217
  390.4 51.3 %copy-start.13 = (pred[6]{0:T(512)(128)(4,1)S(1)}, pred[6]{0:T(512)(128)(4,1)}, u32[]{:S(2)}) copy-start(pred[6]{0:T(512)(128)(4,1)} %copy-done.11) | copy-start | bytes 22
  390.5 51.3 %copy-start.16 = (s32[6]{0:T(128)S(1)}, s32[6]{0:T(128)}, u32[]{:S(2)}) copy-start(s32[6]{0:T(128)} %copy-done.14) | copy-start | bytes 76
  390.5 51.3 %copy-start.19 = (pred[6]{0:T(512)(128)(4,1)S(1)}, pred[6]{0:T(512)(128)(4,1)}, u32[]{:S(2)}) copy-start(pred[6]{0:T(512)(128)(4,1)} %broadcast_compare_fusion) | copy-start | bytes 22
  456.7 1.7 copy-start.8
  492.2 1.5 copy-start.2
Sparse Core Ops, SparseCore 0:
  22.0 121.5 all-gather.3
  218.0 97.1 all-gather.5
  453.2 38.9 reduce-scatter.1
